TPU v7x, 32 devices: a whole 2x2x4 slice. The times are simulated.
32 devices in a mesh: seq: 8 (over z, x), head: 4 (over y, core), batch: 1.
Axes of the slice: x: 2, y: 2, z: 4, core: 2. Of those that a mesh axis runs over, the one named last changes fastest.
Arguments:
- queries: bfloat16 [2048, 4096], P(('batch', 'seq', 'head')), may hold values from -6 to 6
- keys: bfloat16 [2048, 512], P(('batch', 'seq', 'head')), may hold values from -6 to 6
- values: bfloat16 [2048, 512], P(('batch', 'seq', 'head')), may hold values from -6 to 6
- page_of_block: int32 [4], P('batch'), may hold values from 0 to 2, never falling along the last dimension, each value on 1 to 2 neighbouring positions
- links: int32 [4, 4], P('batch'), may hold values 0 or 1
Outputs:
- attended: bfloat16 [2048, 4096], P(('batch', 'seq', 'head'))
Inputs may be any that keep to these rules, and one draw needn't show every extreme that they name: `page_of_block`: page numbers never fall from one block to the next.
All inputs are finite; a program needn't handle non-finite values.
Results may differ from a plain program's by a relative error of at most 0.0065.
Values may be sent and summed in bfloat16 or wider, within the bound.
No kernel may reach another device: no remote copies, remote signals or barrier semaphores. Data moves between devices by JAX's collectives and lax.ppermute only.
A program may use at most 64 MiB of HBM per device.

v0:
```python
import jax
import jax.numpy as jnp
from jax import lax
from jax.sharding import PartitionSpec as P

HEAD_SIZE = 128
BLK = 512


def local(queries, keys, values, page_of_block, links):
    query_all, key_local, value_local = (
        lax.all_to_all(queries, "head", split_axis=1, concat_axis=0, tiled=True),
        lax.all_to_all(keys, "head", split_axis=1, concat_axis=0, tiled=True),
        lax.all_to_all(values, "head", split_axis=1, concat_axis=0, tiled=True),
    )
    row_count = query_all.shape[0]
    kv_here = key_local.shape[1] // HEAD_SIZE
    group_width = query_all.shape[1] // HEAD_SIZE // kv_here
    first_row = lax.axis_index("seq") * row_count
    block_count = page_of_block.shape[0]
    block_ids = jnp.arange(block_count, dtype=jnp.int32)
    page_table = page_of_block.astype(jnp.float32)
    link_table = links.astype(jnp.float32)
    query_pos = first_row + jnp.arange(row_count, dtype=jnp.int32)
    query_onehot = (query_pos[:, None] // BLK == block_ids[None, :]).astype(jnp.float32)
    query_page = jnp.dot(query_onehot, page_table, precision=lax.Precision.HIGHEST)
    query_links = jnp.dot(query_onehot, link_table, precision=lax.Precision.HIGHEST)
    query_heads = query_all.reshape(row_count, kv_here, group_width, HEAD_SIZE)
    score_scale = HEAD_SIZE ** (-0.5)

    def block_step(running, key_block, value_block, offset):
        block_rows = key_block.shape[0]
        key_pos = offset + jnp.arange(block_rows, dtype=jnp.int32)
        key_onehot = (key_pos[:, None] // BLK == block_ids[None, :]).astype(jnp.float32)
        key_page = jnp.dot(key_onehot, page_table, precision=lax.Precision.HIGHEST)
        linked = jnp.dot(query_links, key_onehot.T, precision=lax.Precision.HIGHEST) > 0.5
        same_page = query_page[:, None] == key_page[None, :]
        allowed = jnp.where(same_page, key_pos[None, :] <= query_pos[:, None], linked)

        def attend(previous):
            maxima, totals, weighted = previous
            scores = (
                jnp.einsum(
                    "rkgd,pkd->kgrp",
                    query_heads,
                    key_block.reshape(block_rows, kv_here, HEAD_SIZE),
                    preferred_element_type=jnp.float32,
                )
                * score_scale
            )
            scores = jnp.where(allowed[None, None], scores, -1e30)
            new_max = jnp.maximum(maxima, jnp.max(scores, axis=-1))
            weights = jnp.where(allowed[None, None], jnp.exp(scores - new_max[..., None]), 0.0)
            factor = jnp.exp(maxima - new_max)
            totals = totals * factor + jnp.sum(weights, axis=-1)
            rounded = weights.astype(jnp.bfloat16)
            weighted = weighted * factor[..., None] + jnp.einsum(
                "kgrp,pkd->kgrd",
                rounded,
                value_block.reshape(block_rows, kv_here, HEAD_SIZE),
                preferred_element_type=jnp.float32,
            )
            return (new_max, totals, weighted)

        return lax.cond(jnp.any(allowed), attend, lambda previous: previous, running)

    initial = (
        jnp.full((kv_here, group_width, row_count), -1e30, jnp.float32),
        jnp.zeros((kv_here, group_width, row_count), jnp.float32),
        jnp.zeros((kv_here, group_width, row_count, HEAD_SIZE), jnp.float32),
    )
    running = initial
    key_piece = lax.all_gather(key_local, "seq", axis=0, tiled=True)
    value_piece = lax.all_gather(value_local, "seq", axis=0, tiled=True)
    piece_rows = key_piece.shape[0]
    sub_count = piece_rows // BLK
    key_split = key_piece.reshape(sub_count, BLK, key_piece.shape[1])
    value_split = value_piece.reshape(sub_count, BLK, value_piece.shape[1])

    def scan_step(state_now, scan_item):
        key_block, value_block, block_index = scan_item
        return (block_step(state_now, key_block, value_block, block_index * BLK), None)

    running, unused = lax.scan(
        scan_step, running, (key_split, value_split, jnp.arange(sub_count, dtype=jnp.int32))
    )
    maxima, totals, weighted = running
    outcome = weighted / totals[..., None]
    outcome = (
        outcome.transpose(2, 0, 1, 3)
        .reshape(row_count, kv_here * group_width * HEAD_SIZE)
        .astype(jnp.bfloat16)
    )
    return lax.all_to_all(outcome, "head", split_axis=0, concat_axis=1, tiled=True)


def solution(mesh):
    in_specs = (
        P(("batch", "seq", "head"), None),
        P(("batch", "seq", "head"), None),
        P(("batch", "seq", "head"), None),
        P("batch"),
        P("batch", None),
    )
    out_specs = P(("batch", "seq", "head"), None)
    return jax.shard_map(local, mesh=mesh, in_specs=in_specs, out_specs=out_specs, check_vma=False)
```

profile of v0, /device:TPU:0, one launch (start us, length us, event | category | flops | bytes accessed | tf_op | source)
XLA Modules:
  0.0 122.0 jit_solution(15843513809518971838)
XLA Ops:
  0.0 0.8 copy-done
  0.8 0.6 copy_bitcast_fusion.2
  1.5 4.3 %all-to-all-start = ((bf16[64,4,128]{2,0,1:T(8,128)(2,1)}), bf16[64,4,128]{2,0,1:T(8,128)(2,1)S(1)}, u32[]{:S(2)}, u32[]{:S(2)}) async-start(bf16[64,4,128]{2,0,1:T(8,128)(2,1)} %copy_bitcast_fusion.2), calls=%async_computation | async-start | bytes 131072 | tf_op jit(solution)/shard_map/all_to_all | solution.py:13
  5.8 1.5 %copy_bitcast_fusion.1 = bf16[64,4,128]{2,0,1:T(8,128)(2,1)} fusion(bf16[64,512]{1,0:T(8,128)(2,1)} %param.11), kind=kLoop, calls=%fused_computation.53 | loop fusion | bytes 131072 | tf_op jit(solution)/shard_map/all_to_all | solution.py:14
  7.2 0.9 fusion.41
  8.1 1.7 %all-to-all-done = bf16[64,4,128]{2,0,1:T(8,128)(2,1)S(1)} async-done(((bf16[64,4,128]{2,0,1:T(8,128)(2,1)}), bf16[64,4,128]{2,0,1:T(8,128)(2,1)S(1)}, u32[]{:S(2)}, u32[]{:S(2)}) %all-to-all-start) | async-done | bytes 65568 | tf_op jit(solution)/shard_map/all_to_all | solution.py:13
  9.9 3.3 %all-to-all-start.2 = ((bf16[64,4,128]{2,0,1:T(8,128)(2,1)}), bf16[64,4,128]{2,0,1:T(8,128)(2,1)S(1)}, u32[]{:S(2)}, u32[]{:S(2)}) async-start(bf16[64,4,128]{2,0,1:T(8,128)(2,1)} %copy_bitcast_fusion.1), calls=%async_computation.2 | async-start | bytes 131072 | tf_op jit(solution)/shard_map/all_to_all | solution.py:14
  13.2 0.8 fusion.42
  14.0 0.7 convert_element_type.31
  14.7 1.9 %copy.43 = bf16[8,4,8,1024]{3,2,0,1:T(8,128)(2,1)} copy(bf16[8,4,8,1024]{3,2,1,0:T(8,128)(2,1)} %bitcast.120) | data formatting | bytes 1048576 | tf_op jit(solution)/shard_map/all_to_all | solution.py:12
  17.2 3.5 %all-to-all-start.1 = ((bf16[64,4,1024]{2,0,1:T(8,128)(2,1)}), bf16[64,4,1024]{2,0,1:T(8,128)(2,1)S(1)}, u32[]{:S(2)}, u32[]{:S(2)}) async-start(bf16[64,4,1024]{2,0,1:T(8,128)(2,1)} %bitcast.104), calls=%async_computation.1 | async-start | bytes 1048576 | tf_op jit(solution)/shard_map/all_to_all | solution.py:12
  20.7 32.4 %all_gather.6 = bf16[2048,128]{1,0:T(8,128)(2,1)S(1)} all-gather(bf16[256,128]{1,0:T(8,128)(2,1)S(1)} %bitcast.122), channel_id=1, replica_groups=mesh['seq'=8,'head'=4,'batch'=1] {'seq'}, dimensions={0}, use_global_device_ids=true | all-gather | bytes 589824 | tf_op jit(solution)/shard_map/all_gather | solution.py:73
  53.1 31.2 %all_gather.7 = bf16[2048,128]{1,0:T(8,128)(2,1)S(1)} all-gather(bf16[256,128]{1,0:T(8,128)(2,1)S(1)} %bitcast.123), channel_id=1, replica_groups=mesh['seq'=8,'head'=4,'batch'=1] {'seq'}, dimensions={0}, use_global_device_ids=true | all-gather | bytes 589824 | tf_op jit(solution)/shard_map/all_gather | solution.py:74
  84.5 23.9 %while.19 = (s32[]{:T(128)}, f32[1,8,256]{2,1,0:T(8,128)S(1)}, f32[1,8,256]{2,1,0:T(8,128)S(1)}, f32[1,8,256,128]{3,2,1,0:T(8,128)S(1)}, f32[256]{0:T(256)S(1)},...) while((s32[]{:T(128)}, f32[1,8,256]{2,1,0:T(8,128)S(1)}, ...), condition=%wide.region_6.7_spmd.clone.clone, body=%wide.region_0.6_spmd.clone.clone.sunk | while | flops 558016768 | bytes 16143707 | solution.py:84
  86.1 1.1 fusion.61
  87.9 3.5 %conditional.4 = ((f32[1,8,256]{2,1,0:T(8,128)S(1)}, f32[1,8,256]{2,1,0:T(8,128)S(1)}, f32[1,8,256,128]{3,2,1,0:T(8,128)S(1)})) conditional(s32[]{:T(128)} %convert_element_type.56, (f32[1,8,256]{2,1,0:T(8,128)S(1)}, f32[1,8,256]{2,1,0:T(8,128)S(1)}, f32[1,8,256,128]{3,2,1,0:T(8,128)S(1)}) %tuple.66, (pred[256,512]{0,1:T(8,128)(4,1)S(1)}, ...), branch_computations={%region_2.2_spmd, %region_3.5_spmd} | conditional | flops 551032832 | bytes 15990824 | solution.py:65
  87.9 0.8 fusion.2
  88.7 1.6 %fusion.12 = f32[1,8,256,128]{3,2,1,0:T(8,128)S(1)} fusion(f32[512,256,8]{1,0,2:T(8,128)S(1)} %get-tuple-element.409, f32[8,256]{1,0:T(8,128)S(1)} %bitcast.113, pred[256,512]{0,1:T(8,128)(4,1)S(1)} %get-tuple-element.245, f32[1,8,256,128]{3,2,1,0:T(8,128)S(1)} %get-tuple-element.250, f32[8,256]{1,0:T(8,128)S(1)} %get-tuple-element.406, ...), kind=kOutput, calls=%fused_computation.10 | convolution fusion | flops 274202624 | bytes 6569988 | tf_op jit(solution)/shard_map/while/body/eval_jaxpr/cond/branch_1_fun/kgrp,pkd->kgrd/dot_general | solution.py:57
  90.4 1.0 fusion.4
  93.0 1.1 fusion.61
  94.8 3.5 %conditional.4 = ((f32[1,8,256]{2,1,0:T(8,128)S(1)}, f32[1,8,256]{2,1,0:T(8,128)S(1)}, f32[1,8,256,128]{3,2,1,0:T(8,128)S(1)})) conditional(s32[]{:T(128)} %convert_element_type.56, (f32[1,8,256]{2,1,0:T(8,128)S(1)}, f32[1,8,256]{2,1,0:T(8,128)S(1)}, f32[1,8,256,128]{3,2,1,0:T(8,128)S(1)}) %tuple.66, (pred[256,512]{0,1:T(8,128)(4,1)S(1)}, ...), branch_computations={%region_2.2_spmd, %region_3.5_spmd} | conditional | flops 551032832 | bytes 15990824 | solution.py:65
  94.8 0.8 fusion.2
  95.6 1.6 %fusion.12 = f32[1,8,256,128]{3,2,1,0:T(8,128)S(1)} fusion(f32[512,256,8]{1,0,2:T(8,128)S(1)} %get-tuple-element.409, f32[8,256]{1,0:T(8,128)S(1)} %bitcast.113, pred[256,512]{0,1:T(8,128)(4,1)S(1)} %get-tuple-element.245, f32[1,8,256,128]{3,2,1,0:T(8,128)S(1)} %get-tuple-element.250, f32[8,256]{1,0:T(8,128)S(1)} %get-tuple-element.406, ...), kind=kOutput, calls=%fused_computation.10 | convolution fusion | flops 274202624 | bytes 6569988 | tf_op jit(solution)/shard_map/while/body/eval_jaxpr/cond/branch_1_fun/kgrp,pkd->kgrd/dot_general | solution.py:57
  97.2 1.0 fusion.4
  99.8 1.1 fusion.61
  103.2 1.1 fusion.61
  105.0 3.5 %conditional.4 = ((f32[1,8,256]{2,1,0:T(8,128)S(1)}, f32[1,8,256]{2,1,0:T(8,128)S(1)}, f32[1,8,256,128]{3,2,1,0:T(8,128)S(1)})) conditional(s32[]{:T(128)} %convert_element_type.56, (f32[1,8,256]{2,1,0:T(8,128)S(1)}, f32[1,8,256]{2,1,0:T(8,128)S(1)}, f32[1,8,256,128]{3,2,1,0:T(8,128)S(1)}) %tuple.66, (pred[256,512]{0,1:T(8,128)(4,1)S(1)}, ...), branch_computations={%region_2.2_spmd, %region_3.5_spmd} | conditional | flops 551032832 | bytes 15990824 | solution.py:65
  105.0 0.8 fusion.2
  105.8 1.6 %fusion.12 = f32[1,8,256,128]{3,2,1,0:T(8,128)S(1)} fusion(f32[512,256,8]{1,0,2:T(8,128)S(1)} %get-tuple-element.409, f32[8,256]{1,0:T(8,128)S(1)} %bitcast.113, pred[256,512]{0,1:T(8,128)(4,1)S(1)} %get-tuple-element.245, f32[1,8,256,128]{3,2,1,0:T(8,128)S(1)} %get-tuple-element.250, f32[8,256]{1,0:T(8,128)S(1)} %get-tuple-element.406, ...), kind=kOutput, calls=%fused_computation.10 | convolution fusion | flops 274202624 | bytes 6569988 | tf_op jit(solution)/shard_map/while/body/eval_jaxpr/cond/branch_1_fun/kgrp,pkd->kgrd/dot_general | solution.py:57
  107.4 1.0 fusion.4
  109.4 11.7 %all_to_all.70 = bf16[4,64,1024]{2,1,0:T(8,128)(2,1)S(1)} all-to-all(bf16[4,64,1024]{2,1,0:T(8,128)(2,1)S(1)} %convert_element_type.35), channel_id=1, replica_groups=mesh['seq'=8,'head'=4,'batch'=1] {'head'}, dimensions={0} | all-to-all | bytes 1048576 | tf_op jit(solution)/shard_map/all_to_all | solution.py:94
  121.2 0.8 copy.38
  (39 shorter events, 5.5 us)
Async XLA Ops:
  0.0 0.8 copy-start
  1.5 8.4 %all-to-all-start = ((bf16[64,4,128]{2,0,1:T(8,128)(2,1)}), bf16[64,4,128]{2,0,1:T(8,128)(2,1)S(1)}, u32[]{:S(2)}, u32[]{:S(2)}) async-start(bf16[64,4,128]{2,0,1:T(8,128)(2,1)} %copy_bitcast_fusion.2), calls=%async_computation | async-start | bytes 131072 | tf_op jit(solution)/shard_map/all_to_all | solution.py:13
  9.9 7.4 %all-to-all-start.2 = ((bf16[64,4,128]{2,0,1:T(8,128)(2,1)}), bf16[64,4,128]{2,0,1:T(8,128)(2,1)S(1)}, u32[]{:S(2)}, u32[]{:S(2)}) async-start(bf16[64,4,128]{2,0,1:T(8,128)(2,1)} %copy_bitcast_fusion.1), calls=%async_computation.2 | async-start | bytes 131072 | tf_op jit(solution)/shard_map/all_to_all | solution.py:14
  17.2 67.0 %all-to-all-start.1 = ((bf16[64,4,1024]{2,0,1:T(8,128)(2,1)}), bf16[64,4,1024]{2,0,1:T(8,128)(2,1)S(1)}, u32[]{:S(2)}, u32[]{:S(2)}) async-start(bf16[64,4,1024]{2,0,1:T(8,128)(2,1)} %bitcast.104), calls=%async_computation.1 | async-start | bytes 1048576 | tf_op jit(solution)/shard_map/all_to_all | solution.py:12
where the time goes:
time: 123 us; the launch traced here: 122 us
  blocking collectives  75.2 us (61%)
  matrix products  14.7 us (12%)
  starting transfers between devices  11 us (9%)
  local copies, waits for them, and re-layouts  8.84 us (7%)
  loops' own time  5.51 us (4%)
  other arithmetic  4.22 us (3%)
  waiting for transfers between devices  2.38 us (2%)
    all_gather x1, blocking collectives, local(): key_piece = lax.all_gather(key_local, 'seq', axis=0, tiled=True)  32.4 us
    all_gather x1, blocking collectives, local(): value_piece = lax.all_gather(value_local, 'seq', axis=0, tiled=True)  31.2 us
    all_to_all x1, blocking collectives, local(): lax.all_to_all(outcome, 'head', split_axis=0, concat_axis=1, tiled=True)  11.7 us
    another operation x1, loops' own time, local(): lax.scan(scan_step, running, (key_split, value_split, jnp.arange(sub_coun...  5.34 us
    dot_general x3, matrix products, attend(): jnp.einsum('kgrp,pkd->kgrd', rounded, value_block.reshape(block_rows, kv_...  4.83 us
    dot_general x4, matrix products, block_step(): jnp.dot(query_links, key_onehot.T, precision=lax.Precision.HIGHEST) > 0.5  4.53 us
    all_to_all x1, starting transfers between devices, local(): lax.all_to_all(keys, 'head', split_axis=1, concat_axis=0, tiled=True)  4.26 us
    all_to_all x1, starting transfers between devices, local(): lax.all_to_all(queries, 'head', split_axis=1, concat_axis=0, tiled=True)  3.47 us
  transfers between devices with their start and end apart: 3, of which 2 were waited for; matrix products, arithmetic and copies ran while one was open for 5% of the time, Pallas kernels for 0%

commit v1 on v0

--- a/solution.py
+++ b/solution.py
@@ -2,6 +2,7 @@
 import jax.numpy as jnp
 from jax import lax
 from jax.sharding import PartitionSpec as P
+from jax.lax import all_gather
 
 HEAD_SIZE = 128
 BLK = 512
@@ -70,8 +71,13 @@
         jnp.zeros((kv_here, group_width, row_count, HEAD_SIZE), jnp.float32),
     )
     running = initial
-    key_piece = lax.all_gather(key_local, "seq", axis=0, tiled=True)
-    value_piece = lax.all_gather(value_local, "seq", axis=0, tiled=True)
+    key_piece, value_piece = jnp.split(
+        all_gather(
+            jnp.concatenate([key_local, value_local], axis=1), axis_name="seq", axis=0, tiled=True
+        ),
+        [key_local.shape[1]],
+        axis=1,
+    )
     piece_rows = key_piece.shape[0]
     sub_count = piece_rows // BLK
     key_split = key_piece.reshape(sub_count, BLK, key_piece.shape[1])

time: 123 us -> 111 us (0.902)
  blocking collectives: 75.2 us -> 17.8 us
  waiting for transfers between devices: 2.38 us -> 36.6 us
  between operations: 0.1 us -> 13.5 us
  starting transfers between devices: 11 us -> 7.74 us
    all_gather x2 -> x0, blocking collectives: 63.5 us -> none  [the longest x1 32.4 us: local(): key_piece = lax.all_gather(key_local, 'seq', axis=0, tiled=True)]
    all_gather x0 -> x1, waiting for transfers between devices: none -> 27 us  [local(): all_gather(jnp.concatenate([key_local, value_local], axis=1), axis_name='...]
    all_to_all x0 -> x1, blocking collectives: none -> 6.47 us  [local(): lax.all_to_all(values, 'head', split_axis=1, concat_axis=0, tiled=True)]
    all_to_all x1, waiting for transfers between devices: 0.01 us -> 6.3 us  [local(): lax.all_to_all(queries, 'head', split_axis=1, concat_axis=0, tiled=True)]
    all_to_all x1 -> x0, starting transfers between devices: 3.28 us -> none  [local(): lax.all_to_all(values, 'head', split_axis=1, concat_axis=0, tiled=True)]
    all_to_all x1, waiting for transfers between devices: 1.74 us -> 3.27 us  [local(): lax.all_to_all(keys, 'head', split_axis=1, concat_axis=0, tiled=True)]
    split x0 -> x1, local copies, waits for them, and re-layouts: none -> 1.27 us  [local(): jnp.split(all_gather(jnp.concatenate([key_local, value_local], axis=1), a...]
  transfers between devices with their start and end apart: 3 -> 3, of which waited for: 2 -> 3; matrix products, arithmetic and copies ran while one was open for 5% -> 5% of each run, Pallas kernels for 0% -> 0%
where the time goes in v1:
time: 111 us; the launch traced here: 110 us
  waiting for transfers between devices  36.6 us (33%)
  blocking collectives  17.8 us (16%)
  matrix products  14.7 us (13%)
  between operations  13.5 us (12%)
  local copies, waits for them, and re-layouts  9.48 us (9%)
  starting transfers between devices  7.74 us (7%)
  loops' own time  5.51 us (5%)
  other arithmetic  4.83 us (4%)
    all_gather x1, waiting for transfers between devices, local(): all_gather(jnp.concatenate([key_local, value_local], axis=1), axis_name='...  27 us
    all_to_all x1, blocking collectives, local(): lax.all_to_all(outcome, 'head', split_axis=0, concat_axis=1, tiled=True)  11.4 us
    all_to_all x1, blocking collectives, local(): lax.all_to_all(values, 'head', split_axis=1, concat_axis=0, tiled=True)  6.47 us
    all_to_all x1, waiting for transfers between devices, local(): lax.all_to_all(queries, 'head', split_axis=1, concat_axis=0, tiled=True)  6.3 us
    another operation x1, loops' own time, local(): lax.scan(scan_step, running, (key_split, value_split, jnp.arange(sub_coun...  5.34 us
    dot_general x3, matrix products, attend(): jnp.einsum('kgrp,pkd->kgrd', rounded, value_block.reshape(block_rows, kv_...  4.84 us
    dot_general x4, matrix products, block_step(): jnp.dot(query_links, key_onehot.T, precision=lax.Precision.HIGHEST) > 0.5  4.53 us
    all_to_all x1, starting transfers between devices, local(): lax.all_to_all(keys, 'head', split_axis=1, concat_axis=0, tiled=True)  4.26 us
  transfers between devices with their start and end apart: 3, of which 3 were waited for; matrix products, arithmetic and copies ran while one was open for 5% of the time, Pallas kernels for 0%

profile of v1, /device:TPU:0, one launch (start us, length us, event | category | flops | bytes accessed | tf_op | source)
XLA Modules:
  0.0 110.2 jit_solution(3970051429221018084)
XLA Ops:
  6.5 0.8 copy-done
  8.0 4.3 %all-to-all-start = ((bf16[64,4,128]{2,0,1:T(8,128)(2,1)}), bf16[64,4,128]{2,0,1:T(8,128)(2,1)S(1)}, u32[]{:S(2)}, u32[]{:S(2)}) async-start(bf16[64,4,128]{2,0,1:T(8,128)(2,1)} %copy_bitcast_fusion.2), calls=%async_computation | async-start | bytes 131072 | tf_op jit(solution)/shard_map/all_to_all | solution.py:14
  12.3 0.9 copy_bitcast_fusion.1
  13.1 3.3 %all-to-all-done = bf16[64,4,128]{2,0,1:T(8,128)(2,1)S(1)} async-done(((bf16[64,4,128]{2,0,1:T(8,128)(2,1)}), bf16[64,4,128]{2,0,1:T(8,128)(2,1)S(1)}, u32[]{:S(2)}, u32[]{:S(2)}) %all-to-all-start) | async-done | bytes 65568 | tf_op jit(solution)/shard_map/all_to_all | solution.py:14
  16.4 6.5 %all_to_all.70 = bf16[64,4,128]{2,0,1:T(8,128)(2,1)S(1)} all-to-all(bf16[64,4,128]{2,0,1:T(8,128)(2,1)S(1)} %copy_bitcast_fusion.1), channel_id=1, replica_groups=mesh['seq'=8,'head'=4,'batch'=1] {'head'}, dimensions={1} | all-to-all | bytes 131072 | tf_op jit(solution)/shard_map/all_to_all | solution.py:15
  22.9 0.7 pad_maximum_fusion
  23.6 1.9 %copy.43 = bf16[8,4,8,1024]{3,2,0,1:T(8,128)(2,1)} copy(bf16[8,4,8,1024]{3,2,1,0:T(8,128)(2,1)} %bitcast.119) | data formatting | bytes 1048576 | tf_op jit(solution)/shard_map/all_to_all | solution.py:13
  25.5 3.5 %all-to-all-start.2 = ((bf16[64,4,1024]{2,0,1:T(8,128)(2,1)}), bf16[64,4,1024]{2,0,1:T(8,128)(2,1)S(1)}, u32[]{:S(2)}, u32[]{:S(2)}) async-start(bf16[64,4,1024]{2,0,1:T(8,128)(2,1)} %bitcast.104), calls=%async_computation.2 | async-start | bytes 1048576 | tf_op jit(solution)/shard_map/all_to_all | solution.py:13
  29.6 0.9 fusion.42
  30.5 0.9 fusion.41
  31.4 6.3 %all-to-all-done.2 = bf16[64,4,1024]{2,0,1:T(8,128)(2,1)S(1)} async-done(((bf16[64,4,1024]{2,0,1:T(8,128)(2,1)}), bf16[64,4,1024]{2,0,1:T(8,128)(2,1)S(1)}, u32[]{:S(2)}, u32[]{:S(2)}) %all-to-all-start.2) | async-done | bytes 524320 | tf_op jit(solution)/shard_map/all_to_all | solution.py:13
  37.9 27.0 %all-gather.2.cloned.1.call-done = bf16[2048,256]{1,0:T(8,128)(2,1)} async-done(((bf16[256,256]{1,0:T(8,128)(2,1)}), bf16[2048,256]{1,0:T(8,128)(2,1)}) %all-gather.2.cloned.1.call-update) | async-done | bytes 1048592 | tf_op jit(solution)/shard_map/all_gather | solution.py:75
  64.9 1.3 %fusion.49 = (bf16[2048,128]{1,0:T(8,128)(2,1)S(1)}, bf16[2048,128]{1,0:T(8,128)(2,1)S(1)}) fusion(bf16[2048,256]{1,0:T(8,128)(2,1)} %all-gather.2.cloned.1.call-done), kind=kLoop, calls=%fused_computation.66 | loop fusion | bytes 2097152 | tf_op jit(solution)/shard_map/split | solution.py:74
  66.3 24.0 %while.19 = (s32[]{:T(128)}, f32[1,8,256]{2,1,0:T(8,128)S(1)}, f32[1,8,256]{2,1,0:T(8,128)S(1)}, f32[1,8,256,128]{3,2,1,0:T(8,128)S(1)}, f32[256]{0:T(256)S(1)},...) while((s32[]{:T(128)}, f32[1,8,256]{2,1,0:T(8,128)S(1)}, ...), condition=%wide.region_6.7_spmd.clone.clone, body=%wide.region_0.6_spmd.clone.clone.sunk | while | flops 558016768 | bytes 16143707 | solution.py:90
  67.9 1.1 %fusion.62 = (pred[]{:T(512)}, pred[256,512]{0,1:T(8,128)(4,1)S(1)}) fusion(f32[256,4]{0,1:T(4,128)S(1)} %get-tuple-element.544, s32[4]{0:T(128)S(1)} %get-tuple-element.542, s32[512]{0:T(512)S(1)} %get-tuple-element.496, s32[256]{0:T(256)S(1)} %iota_add_fusion.3, s32[512]{0:T(512)S(1)} %get-tuple-element.497, f32[512]{0:T(512)S(1)} %bitcast.124, ...), kind=kOutput, calls=%fused_computation.65.clone.1 | convolution fusion | flops 6948863 | bytes 143377 | tf_op jit(solution)/shard_map/while/body/eval_jaxpr/dot_general | solution.py:37
  69.6 3.5 %conditional.4 = ((f32[1,8,256]{2,1,0:T(8,128)S(1)}, f32[1,8,256]{2,1,0:T(8,128)S(1)}, f32[1,8,256,128]{3,2,1,0:T(8,128)S(1)})) conditional(s32[]{:T(128)} %convert_element_type.56, (f32[1,8,256]{2,1,0:T(8,128)S(1)}, f32[1,8,256]{2,1,0:T(8,128)S(1)}, f32[1,8,256,128]{3,2,1,0:T(8,128)S(1)}) %tuple.67, (pred[256,512]{0,1:T(8,128)(4,1)S(1)}, ...), branch_computations={%region_2.2_spmd, %region_3.5_spmd} | conditional | flops 551032832 | bytes 15990824 | solution.py:66
  69.7 0.8 fusion.2
  70.5 1.6 %fusion.12 = f32[1,8,256,128]{3,2,1,0:T(8,128)S(1)} fusion(f32[512,256,8]{1,0,2:T(8,128)S(1)} %get-tuple-element.409, f32[8,256]{1,0:T(8,128)S(1)} %bitcast.113, pred[256,512]{0,1:T(8,128)(4,1)S(1)} %get-tuple-element.245, f32[1,8,256,128]{3,2,1,0:T(8,128)S(1)} %get-tuple-element.250, f32[8,256]{1,0:T(8,128)S(1)} %get-tuple-element.406, ...), kind=kOutput, calls=%fused_computation.10 | convolution fusion | flops 274202624 | bytes 6569988 | tf_op jit(solution)/shard_map/while/body/eval_jaxpr/cond/branch_1_fun/kgrp,pkd->kgrd/dot_general | solution.py:58
  72.1 1.0 fusion.4
  74.7 1.1 %fusion.62 = (pred[]{:T(512)}, pred[256,512]{0,1:T(8,128)(4,1)S(1)}) fusion(f32[256,4]{0,1:T(4,128)S(1)} %get-tuple-element.544, s32[4]{0:T(128)S(1)} %get-tuple-element.542, s32[512]{0:T(512)S(1)} %get-tuple-element.496, s32[256]{0:T(256)S(1)} %iota_add_fusion.3, s32[512]{0:T(512)S(1)} %get-tuple-element.497, f32[512]{0:T(512)S(1)} %bitcast.124, ...), kind=kOutput, calls=%fused_computation.65.clone.1 | convolution fusion | flops 6948863 | bytes 143377 | tf_op jit(solution)/shard_map/while/body/eval_jaxpr/dot_general | solution.py:37
  76.5 3.5 %conditional.4 = ((f32[1,8,256]{2,1,0:T(8,128)S(1)}, f32[1,8,256]{2,1,0:T(8,128)S(1)}, f32[1,8,256,128]{3,2,1,0:T(8,128)S(1)})) conditional(s32[]{:T(128)} %convert_element_type.56, (f32[1,8,256]{2,1,0:T(8,128)S(1)}, f32[1,8,256]{2,1,0:T(8,128)S(1)}, f32[1,8,256,128]{3,2,1,0:T(8,128)S(1)}) %tuple.67, (pred[256,512]{0,1:T(8,128)(4,1)S(1)}, ...), branch_computations={%region_2.2_spmd, %region_3.5_spmd} | conditional | flops 551032832 | bytes 15990824 | solution.py:66
  76.5 0.8 fusion.2
  77.3 1.6 %fusion.12 = f32[1,8,256,128]{3,2,1,0:T(8,128)S(1)} fusion(f32[512,256,8]{1,0,2:T(8,128)S(1)} %get-tuple-element.409, f32[8,256]{1,0:T(8,128)S(1)} %bitcast.113, pred[256,512]{0,1:T(8,128)(4,1)S(1)} %get-tuple-element.245, f32[1,8,256,128]{3,2,1,0:T(8,128)S(1)} %get-tuple-element.250, f32[8,256]{1,0:T(8,128)S(1)} %get-tuple-element.406, ...), kind=kOutput, calls=%fused_computation.10 | convolution fusion | flops 274202624 | bytes 6569988 | tf_op jit(solution)/shard_map/while/body/eval_jaxpr/cond/branch_1_fun/kgrp,pkd->kgrd/dot_general | solution.py:58
  78.9 1.0 fusion.4
  81.6 1.1 %fusion.62 = (pred[]{:T(512)}, pred[256,512]{0,1:T(8,128)(4,1)S(1)}) fusion(f32[256,4]{0,1:T(4,128)S(1)} %get-tuple-element.544, s32[4]{0:T(128)S(1)} %get-tuple-element.542, s32[512]{0:T(512)S(1)} %get-tuple-element.496, s32[256]{0:T(256)S(1)} %iota_add_fusion.3, s32[512]{0:T(512)S(1)} %get-tuple-element.497, f32[512]{0:T(512)S(1)} %bitcast.124, ...), kind=kOutput, calls=%fused_computation.65.clone.1 | convolution fusion | flops 6948863 | bytes 143377 | tf_op jit(solution)/shard_map/while/body/eval_jaxpr/dot_general | solution.py:37
  85.0 1.1 %fusion.62 = (pred[]{:T(512)}, pred[256,512]{0,1:T(8,128)(4,1)S(1)}) fusion(f32[256,4]{0,1:T(4,128)S(1)} %get-tuple-element.544, s32[4]{0:T(128)S(1)} %get-tuple-element.542, s32[512]{0:T(512)S(1)} %get-tuple-element.496, s32[256]{0:T(256)S(1)} %iota_add_fusion.3, s32[512]{0:T(512)S(1)} %get-tuple-element.497, f32[512]{0:T(512)S(1)} %bitcast.124, ...), kind=kOutput, calls=%fused_computation.65.clone.1 | convolution fusion | flops 6948863 | bytes 143377 | tf_op jit(solution)/shard_map/while/body/eval_jaxpr/dot_general | solution.py:37
  86.7 3.5 %conditional.4 = ((f32[1,8,256]{2,1,0:T(8,128)S(1)}, f32[1,8,256]{2,1,0:T(8,128)S(1)}, f32[1,8,256,128]{3,2,1,0:T(8,128)S(1)})) conditional(s32[]{:T(128)} %convert_element_type.56, (f32[1,8,256]{2,1,0:T(8,128)S(1)}, f32[1,8,256]{2,1,0:T(8,128)S(1)}, f32[1,8,256,128]{3,2,1,0:T(8,128)S(1)}) %tuple.67, (pred[256,512]{0,1:T(8,128)(4,1)S(1)}, ...), branch_computations={%region_2.2_spmd, %region_3.5_spmd} | conditional | flops 551032832 | bytes 15990824 | solution.py:66
  86.8 0.8 fusion.2
  87.6 1.6 %fusion.12 = f32[1,8,256,128]{3,2,1,0:T(8,128)S(1)} fusion(f32[512,256,8]{1,0,2:T(8,128)S(1)} %get-tuple-element.409, f32[8,256]{1,0:T(8,128)S(1)} %bitcast.113, pred[256,512]{0,1:T(8,128)(4,1)S(1)} %get-tuple-element.245, f32[1,8,256,128]{3,2,1,0:T(8,128)S(1)} %get-tuple-element.250, f32[8,256]{1,0:T(8,128)S(1)} %get-tuple-element.406, ...), kind=kOutput, calls=%fused_computation.10 | convolution fusion | flops 274202624 | bytes 6569988 | tf_op jit(solution)/shard_map/while/body/eval_jaxpr/cond/branch_1_fun/kgrp,pkd->kgrd/dot_general | solution.py:58
  89.2 1.0 fusion.4
  91.2 11.4 %all_to_all.71 = bf16[4,64,1024]{2,1,0:T(8,128)(2,1)S(1)} all-to-all(bf16[4,64,1024]{2,1,0:T(8,128)(2,1)S(1)} %convert_element_type.35), channel_id=1, replica_groups=mesh['seq'=8,'head'=4,'batch'=1] {'head'}, dimensions={0} | all-to-all | bytes 1048576 | tf_op jit(solution)/shard_map/all_to_all | solution.py:100
  102.5 0.8 copy.38
  (41 shorter events, 6.2 us)
Async XLA Ops:
  6.5 0.8 copy-start
  8.0 8.4 %all-to-all-start = ((bf16[64,4,128]{2,0,1:T(8,128)(2,1)}), bf16[64,4,128]{2,0,1:T(8,128)(2,1)S(1)}, u32[]{:S(2)}, u32[]{:S(2)}) async-start(bf16[64,4,128]{2,0,1:T(8,128)(2,1)} %copy_bitcast_fusion.2), calls=%async_computation | async-start | bytes 131072 | tf_op jit(solution)/shard_map/all_to_all | solution.py:14
  12.3 52.6 %all-gather.2.cloned.1.call-start = ((), (), s32[]{:S(2)}) async-start(), calls=%async_computation.4 | async-start | bytes 1179648 | tf_op jit(solution)/shard_map/all_gather | solution.py:75
  25.5 12.3 %all-to-all-start.2 = ((bf16[64,4,1024]{2,0,1:T(8,128)(2,1)}), bf16[64,4,1024]{2,0,1:T(8,128)(2,1)S(1)}, u32[]{:S(2)}, u32[]{:S(2)}) async-start(bf16[64,4,1024]{2,0,1:T(8,128)(2,1)} %bitcast.104), calls=%async_computation.2 | async-start | bytes 1048576 | tf_op jit(solution)/shard_map/all_to_all | solution.py:13
Sparse Core Ops, SparseCore 0:
  23.7 41.1 all-gather.1
